TPU v7x, 512 devices: a whole 4x8x8 slice. The times are simulated.
512 devices in a mesh: dp: 16 (over x, z_hi), code: 32 (over z_lo, y, core).
Axes of the slice: x: 4, y: 8, z: 8 (z_hi: 4, z_lo: 2; z = z_hi * 2 + z_lo), core: 2. Of those that a mesh axis runs over, the one named last changes fastest.
Arguments:
- tokens: bfloat16 [8192, 256], P('dp'), may hold values from -40 to 40
- codebook: bfloat16 [131072, 256], P('code'), may hold values from -6 to 6
- cotangent: bfloat16 [8192, 256], P('dp'), may hold values from -6 to 6
- index: int32 [8192], P('dp'), may hold values from 0 to 131071
Outputs:
- quantized: bfloat16 [8192, 256], P('dp')
- token_grad: bfloat16 [8192, 256], P('dp')
- codebook_grad: bfloat16 [131072, 256], P(('code', 'dp'))
- code_usage: float32 [131072], P(('code', 'dp'))
- entropy_loss: float32 [], replicated
All inputs are finite; a program needn't handle non-finite values.
Results may differ from a plain program's by a relative error of at most 0.012.
Values may be sent and summed in bfloat16 or wider, within the bound.
A program may use at most 64 MiB of HBM per device.

v0:
```python
import jax
import jax.numpy as jnp
from jax import lax
from jax.sharding import PartitionSpec as P


def body(tokens, codebook, cotangent, index):
    token_rows, features = tokens.shape
    code_rows = codebook.shape[0]
    scale_factor = float(features) ** (-0.5)
    code_devices = lax.axis_size("code")
    data_devices = lax.axis_size("dp")
    offset = lax.axis_index("code") * code_rows
    block_length = min(1024, code_rows)
    block_count = code_rows // block_length
    stacked = codebook.reshape(block_count, block_length, features)
    local_ids = index - offset
    inside = (local_ids >= 0) & (local_ids < code_rows)
    picked = jnp.take(codebook, jnp.where(inside, local_ids, 0), axis=0)
    picked = jnp.where(inside[:, None], picked.astype(jnp.float32), 0.0)
    quantized = lax.psum(picked.astype(jnp.bfloat16), "code")
    chosen_sums = jax.ops.segment_sum(
        cotangent.astype(jnp.float32),
        jnp.where(inside, local_ids, code_rows),
        num_segments=code_rows + 1,
    )[:code_rows]

    def scores(code_block):
        logits = (
            jnp.einsum("td,kd->tk", tokens, code_block, preferred_element_type=jnp.float32)
            * scale_factor
        )
        sensed = jnp.einsum("td,kd->tk", cotangent, code_block, preferred_element_type=jnp.float32)
        return (logits, sensed)

    def block_totals(code_block):
        logits, sensed = scores(code_block)
        row_top = jnp.max(logits, axis=1)
        weights = jnp.exp(logits - row_top[:, None])
        return (
            row_top,
            jnp.sum(weights, axis=1),
            jnp.sum(weights * sensed, axis=1),
            jnp.sum(weights * logits, axis=1),
        )

    block_tops, block_sums, sensed_sums, logit_sums = lax.map(block_totals, stacked)
    local_peak = jnp.max(block_tops, axis=0)
    factor = jnp.exp(block_tops - local_peak[None, :])
    local_stats = (
        local_peak,
        jnp.sum(block_sums * factor, axis=0),
        jnp.sum(sensed_sums * factor, axis=0),
        jnp.sum(logit_sums * factor, axis=0),
    )
    row_peak = lax.pmax(local_stats[0], "code")
    rescale = jnp.exp(local_stats[0] - row_peak)
    row_total, sensed_total, logit_total = lax.psum(
        (local_stats[1] * rescale, local_stats[2] * rescale, local_stats[3] * rescale), "code"
    )
    row_dot = sensed_total / row_total
    token_entropy = jnp.log(row_total) + row_peak - logit_total / row_total

    def block_grads(code_block):
        logits, sensed = scores(code_block)
        probs = jnp.exp(logits - row_peak[:, None]) / row_total[:, None]
        logit_grad = (probs * (sensed - row_dot[:, None])).astype(jnp.bfloat16)
        return (probs, logit_grad)

    def gradient_step(running, code_block):
        probs, logit_grad = block_grads(code_block)
        running = running + jnp.dot(logit_grad, code_block, preferred_element_type=jnp.float32)
        usage_part = jnp.sum(probs, axis=0)
        grad_term = scale_factor * jnp.einsum(
            "tk,td->kd", logit_grad, tokens, preferred_element_type=jnp.float32
        )
        return (running, (usage_part, grad_term))

    running, outputs = lax.scan(
        gradient_step, jnp.zeros((token_rows, features), jnp.float32), stacked
    )
    usage_local = outputs[0].reshape(code_rows)
    code_local = outputs[1].reshape(code_rows, features) + chosen_sums
    code_sum = lax.psum_scatter(
        code_local.astype(jnp.bfloat16), "dp", scatter_dimension=0, tiled=True
    )
    usage_sum = lax.psum_scatter(usage_local, "dp", scatter_dimension=0, tiled=True)
    token_grad = (lax.psum(running, "code") * scale_factor).astype(jnp.bfloat16)
    tokens_total = token_rows * data_devices
    codes_total = code_rows * code_devices
    code_usage = usage_sum * (codes_total / tokens_total)
    shares = usage_sum / tokens_total
    local_loss = jnp.sum(token_entropy) / (tokens_total * code_devices) + jnp.sum(
        jax.scipy.special.xlogy(shares, shares)
    )
    entropy_loss = lax.psum(local_loss, ("dp", "code"))
    return (quantized, token_grad, code_sum, code_usage, entropy_loss)


def solution(mesh):
    placed = (P("dp", None), P("code", None), P("dp", None), P("dp"))
    return jax.shard_map(
        body,
        mesh=mesh,
        in_specs=placed,
        out_specs=(P("dp", None), P("dp", None), P(("code", "dp"), None), P(("code", "dp")), P()),
        check_vma=False,
    )
```

profile of v0, /device:TPU:1, one launch (start us, length us, event | category | flops | bytes accessed | tf_op | source)
XLA Modules:
  0.0 632.0 jit_solution(5439487695934471928)
XLA Ops:
  8.0 0.0 all-reduce.7.cloned.1.call-start
  8.1 16.1 %while.31 = (s32[]{:T(128)}, f32[4,512]{1,0:T(4,128)S(1)}, f32[4,512]{1,0:T(4,128)S(1)}, f32[4,512]{1,0:T(4,128)S(1)}, f32[4,512]{1,0:T(4,128)S(1)}, /*index=5*/...) while((s32[]{:T(128)}, f32[4,512]{1,0:T(4,128)S(1)}, ...), condition=%wide.region_6.7_spmd, body=%wide.region_1.0_spmd.sunk | while | flops 542636032 | bytes 8941729 | solution.py:47
  8.1 1.6 multiply_reduce_fusion.5
  9.8 1.6 fusion.56
  11.4 0.5 fusion.55
  12.0 0.1 dynamic_update_slice.33
  12.0 0.1 dynamic_update_slice.31
  12.1 0.1 dynamic_update_slice.30
  12.2 1.6 multiply_reduce_fusion.5
  13.8 1.6 fusion.56
  15.4 0.5 fusion.55
  16.0 0.1 dynamic_update_slice.33
  16.1 0.1 dynamic_update_slice.31
  16.1 0.1 dynamic_update_slice.30
  16.2 1.6 multiply_reduce_fusion.5
  17.8 1.6 fusion.56
  19.4 0.5 fusion.55
  20.0 0.1 dynamic_update_slice.33
  20.1 0.1 dynamic_update_slice.31
  20.1 0.1 dynamic_update_slice.30
  20.2 1.6 multiply_reduce_fusion.5
  21.9 1.6 fusion.56
  23.5 0.5 fusion.55
  24.0 0.1 dynamic_update_slice.33
  24.1 0.1 dynamic_update_slice.31
  24.2 0.1 dynamic_update_slice.30
  24.2 59.2 %pmax.7 = f32[512]{0:T(512)S(1)} all-reduce(f32[512]{0:T(512)S(1)} %reduce_max.18), channel_id=1, replica_groups=mesh['dp'=16,'code'=32] {'code'}, use_global_device_ids=true, to_apply=%region_8.9 | all-reduce | flops 512 | bytes 4096 | tf_op jit(solution)/shard_map/pmax | solution.py:56
  83.5 53.9 %all-reduce.1 = (f32[512]{0:T(512)S(1)}, f32[512]{0:T(512)S(1)}, f32[512]{0:T(512)S(1)}) all-reduce(f32[512]{0:T(512)S(1)} %get-tuple-element.198, f32[512]{0:T(512)S(1)} %get-tuple-element.197, f32[512]{0:T(512)S(1)} %get-tuple-element.196), channel_id=1, replica_groups=mesh['dp'=16,'code'=32] {'code'}, use_global_device_ids=true, to_apply=%region_10.11 | all-reduce | flops 1536 | bytes 12288 | tf_op jit(solution)/shard_map/psum | solution.py:58
  137.4 0.6 subtract_reduce_fusion
  138.0 24.0 %while.32 = (s32[]{:T(128)}, f32[512,256]{1,0:T(8,128)}, f32[4,1024]{1,0:T(4,128)S(1)}, f32[4,1024,256]{2,1,0:T(8,128)}, bf16[4,1024,256]{2,1,0:T(8,128)(2,1)}, ...) while((s32[]{:T(128)}, f32[512,256]{1,0:T(8,128)}, ...), condition=%wide.region_15.16_spmd.clone, body=%wide.region_13.15_spmd.clone.sunk | while | flops 1077935104 | bytes 22300912 | solution.py:79
  138.0 1.9 fusion.64
  140.0 0.5 multiply_convert_fusion.3
  140.5 0.1 dynamic_update_slice.35
  140.6 1.2 convolution_add_fusion.2
  141.8 1.5 fusion.65
  143.3 1.9 fusion.64
  145.2 0.5 multiply_convert_fusion.3
  145.7 0.1 dynamic_update_slice.35
  145.8 2.3 convolution_add_fusion.2
  148.1 1.4 fusion.65
  149.5 1.9 fusion.64
  151.5 0.5 multiply_convert_fusion.3
  152.0 0.1 dynamic_update_slice.35
  152.0 2.3 convolution_add_fusion.2
  154.3 1.5 fusion.65
  155.8 1.9 fusion.64
  157.7 0.5 multiply_convert_fusion.3
  158.2 0.1 dynamic_update_slice.35
  158.3 2.3 convolution_add_fusion.2
  160.6 1.4 fusion.65
  162.1 0.0 all-reduce.5.cloned.1.call-start
  162.2 3.4 gather_fusion
  165.6 0.9 select_convert_fusion
  166.5 0.0 reduce-scatter.2.cloned.1.call-start
  166.6 6.4 %scatter_custom_fusion = f32[4097,256]{1,0:T(8,128)} fusion(s32[512]{0:T(512)S(1)} %subtract_select_fusion, f32[]{:T(128)} %constant.46.clone.1, bf16[512,256]{1,0:T(8,128)(2,1)S(1)} %copy-done.3), kind=kCustom, calls=%fused_computation.34 | custom fusion | flops 262144 | bytes 4457476 | tf_op jit(solution)/shard_map/scatter-add | solution.py:22
  173.0 5.3 fusion.22
  178.3 1.3 dynamic-slice
  180.9 72.7 %all-reduce = f32[4096]{0:T(1024)S(1)} all-reduce(f32[4096]{0:T(1024)S(1)} %bitcast.105), channel_id=3, replica_groups=mesh['dp'=16,'code'=32] {'dp'}, use_global_device_ids=true, to_apply=%region_19.20.clone | all-reduce | flops 4096 | bytes 32768
  253.6 1.2 fusion.26
  255.4 107.1 %psum.47 = f32[]{:T(128)} all-reduce(f32[]{:T(128)S(6)} %add.45), channel_id=1, replica_groups=mesh['dp'=16,'code'=32] {'dp','code'}, use_global_device_ids=true, to_apply=%region_24.25 | all-reduce | flops 1 | bytes 8 | tf_op jit(solution)/shard_map/psum | solution.py:96
  362.5 28.9 %all-reduce.7.cloned.1.call-done = f32[512,256]{1,0:T(8,128)} async-done(((f32[512,256]{1,0:T(8,128)}), f32[512,256]{1,0:T(8,128)}) %all-reduce.7.cloned.1.call-update) | async-done | bytes 524304 | tf_op jit(solution)/shard_map/psum | solution.py:88
  391.4 1.8 multiply_convert_fusion.1
  393.2 229.7 %all-reduce.5.cloned.1.call-done = bf16[512,256]{1,0:T(8,128)(2,1)} async-done(((bf16[512,256]{1,0:T(8,128)(2,1)}), bf16[512,256]{1,0:T(8,128)(2,1)}) %all-reduce.5.cloned.1.call-update) | async-done | bytes 262160 | tf_op jit(solution)/shard_map/psum | solution.py:21
  622.9 1.7 copy.51
  (58 shorter events, 0.4 us)
Async XLA Ops:
  8.0 383.4 %all-reduce.7.cloned.1.call-start = ((), (), s32[]{:S(2)}) async-start(), calls=%async_computation.2 | async-start | bytes 1048576 | tf_op jit(solution)/shard_map/psum | solution.py:88
  8.1 1.6 copy-start.1
  12.1 1.6 copy-start.1
  16.2 1.6 copy-start.1
  20.2 1.7 copy-start.1
  138.0 24.1 %copy-start.5 = (s32[512]{0:T(512)S(1)}, s32[512]{0:T(512)}, u32[]{:S(2)}) copy-start(s32[512]{0:T(512)} %param.11) | copy-start | bytes 6148
  138.0 1.9 copy-start
  138.0 1.9 copy-start.2
  140.5 1.3 copy-start.4
  143.3 1.9 copy-start
  143.3 1.9 copy-start.2
  145.7 2.4 copy-start.4
  149.5 1.9 copy-start
  149.5 1.9 copy-start.2
  151.9 2.4 copy-start.4
  155.8 1.9 copy-start
  155.8 1.9 copy-start.2
  158.2 2.4 copy-start.4
  162.0 4.6 copy-start.3
  162.1 460.8 %all-reduce.5.cloned.1.call-start = ((), (), s32[]{:S(2)}) async-start(), calls=%async_computation.1 | async-start | bytes 524288 | tf_op jit(solution)/shard_map/psum | solution.py:21
  166.5 456.4 %reduce-scatter.2.cloned.1.call-start = ((), (), s32[]{:S(2)}) async-start(), calls=%async_computation.3 | async-start | bytes 2228224 | tf_op jit(solution)/shard_map/reduce_scatter | solution.py:84
Sparse Core Ops, SparseCore 0:
  162.2 229.1 all-reduce.6
  394.9 227.9 all-reduce.4
Sparse Core Ops, SparseCore 1:
  178.4 91.6 reduce-scatter.1
where the time goes:
time: 633 us; the launch traced here: 632 us
  blocking collectives  293 us (46%)
  waiting for transfers between devices  259 us (41%)
  matrix products  36.4 us (6%)
  other arithmetic  18.4 us (3%)
  between operations  17.6 us (3%)
  local copies, waits for them, and re-layouts  7.52 us (1%)
    psum x1, waiting for transfers between devices, body(): quantized = lax.psum(picked.astype(jnp.bfloat16), 'code')  230 us
    psum x1, blocking collectives, body(): entropy_loss = lax.psum(local_loss, ('dp', 'code'))  107 us
    unnamed x1, blocking collectives  72.7 us
    pmax x1, blocking collectives, body(): row_peak = lax.pmax(local_stats[0], 'code')  59.2 us
    psum x1, blocking collectives, body(): lax.psum((local_stats[1] * rescale, local_stats[2] * rescale, local_stats...  53.9 us
    psum x1, waiting for transfers between devices, body(): token_grad = (lax.psum(running, 'code') * scale_factor).astype(jnp.bfloat16)  28.9 us
    dot_general x8, matrix products, scores(): jnp.einsum('td,kd->tk', tokens, code_block, preferred_element_type=jnp.fl...  14.2 us
  transfers between devices with their start and end apart: 3, of which 2 were waited for; matrix products, arithmetic and copies ran while one was open for 3% of the time, Pallas kernels for 0%

commit v1 on v0

--- a/solution.py
+++ b/solution.py
@@ -18,7 +18,7 @@
     inside = (local_ids >= 0) & (local_ids < code_rows)
     picked = jnp.take(codebook, jnp.where(inside, local_ids, 0), axis=0)
     picked = jnp.where(inside[:, None], picked.astype(jnp.float32), 0.0)
-    quantized = lax.psum(picked.astype(jnp.bfloat16), "code")
+    quantized = jnp.sum(lax.all_gather(picked.astype(jnp.bfloat16), "code"), axis=0)
     chosen_sums = jax.ops.segment_sum(
         cotangent.astype(jnp.float32),
         jnp.where(inside, local_ids, code_rows),

time: 633 us -> 482 us (0.76)
  waiting for transfers between devices: 259 us -> 104 us
    psum x1 -> x0, waiting for transfers between devices: 230 us -> none  [body(): quantized = lax.psum(picked.astype(jnp.bfloat16), 'code')]
    all_gather x0 -> x1, waiting for transfers between devices: none -> 74.7 us  [body(): lax.all_gather(picked.astype(jnp.bfloat16), 'code')]
  transfers between devices with their start and end apart: 3 -> 3, of which waited for: 2 -> 2; matrix products, arithmetic and copies ran while one was open for 3% -> 5% of each run, Pallas kernels for 0% -> 0%
where the time goes in v1:
time: 482 us; the launch traced here: 481 us
  blocking collectives  293 us (61%)
  waiting for transfers between devices  104 us (22%)
  matrix products  36.4 us (8%)
  other arithmetic  23.7 us (5%)
  between operations  17.6 us (4%)
  local copies, waits for them, and re-layouts  5.86 us (1%)
    psum x1, blocking collectives, body(): entropy_loss = lax.psum(local_loss, ('dp', 'code'))  106 us
    all_gather x1, waiting for transfers between devices, body(): lax.all_gather(picked.astype(jnp.bfloat16), 'code')  74.7 us
    unnamed x1, blocking collectives  73.5 us
    pmax x1, blocking collectives, body(): row_peak = lax.pmax(local_stats[0], 'code')  59.2 us
    psum x1, blocking collectives, body(): lax.psum((local_stats[1] * rescale, local_stats[2] * rescale, local_stats...  53.9 us
    psum x1, waiting for transfers between devices, body(): token_grad = (lax.psum(running, 'code') * scale_factor).astype(jnp.bfloat16)  29 us
    dot_general x8, matrix products, scores(): jnp.einsum('td,kd->tk', tokens, code_block, preferred_element_type=jnp.fl...  14.2 us
  transfers between devices with their start and end apart: 3, of which 2 were waited for; matrix products, arithmetic and copies ran while one was open for 5% of the time, Pallas kernels for 0%

profile of v1, /device:TPU:1, one launch (start us, length us, event | category | flops | bytes accessed | tf_op | source)
XLA Modules:
  0.0 481.0 jit_solution(11857187358249123040)
XLA Ops:
  8.0 0.0 all-reduce.4.cloned.1.call-start
  8.1 16.1 %while.31 = (s32[]{:T(128)}, f32[4,512]{1,0:T(4,128)S(1)}, f32[4,512]{1,0:T(4,128)S(1)}, f32[4,512]{1,0:T(4,128)S(1)}, f32[4,512]{1,0:T(4,128)S(1)}, /*index=5*/...) while((s32[]{:T(128)}, f32[4,512]{1,0:T(4,128)S(1)}, ...), condition=%wide.region_6.7_spmd, body=%wide.region_1.0_spmd.sunk | while | flops 542636032 | bytes 8941729 | solution.py:47
  8.1 1.6 multiply_reduce_fusion.5
  9.8 1.6 fusion.56
  11.4 0.5 fusion.55
  12.0 0.1 dynamic_update_slice.33
  12.0 0.1 dynamic_update_slice.31
  12.1 0.1 dynamic_update_slice.30
  12.2 1.6 multiply_reduce_fusion.5
  13.8 1.6 fusion.56
  15.4 0.5 fusion.55
  16.0 0.1 dynamic_update_slice.33
  16.1 0.1 dynamic_update_slice.31
  16.1 0.1 dynamic_update_slice.30
  16.2 1.6 multiply_reduce_fusion.5
  17.8 1.6 fusion.56
  19.4 0.5 fusion.55
  20.0 0.1 dynamic_update_slice.33
  20.1 0.1 dynamic_update_slice.31
  20.1 0.1 dynamic_update_slice.30
  20.2 1.6 multiply_reduce_fusion.5
  21.9 1.6 fusion.56
  23.5 0.5 fusion.55
  24.0 0.1 dynamic_update_slice.33
  24.1 0.1 dynamic_update_slice.31
  24.2 0.1 dynamic_update_slice.30
  24.2 59.2 %pmax.7 = f32[512]{0:T(512)S(1)} all-reduce(f32[512]{0:T(512)S(1)} %reduce_max.18), channel_id=1, replica_groups=mesh['dp'=16,'code'=32] {'code'}, use_global_device_ids=true, to_apply=%region_8.9 | all-reduce | flops 512 | bytes 4096 | tf_op jit(solution)/shard_map/pmax | solution.py:56
  83.5 53.9 %all-reduce.1 = (f32[512]{0:T(512)S(1)}, f32[512]{0:T(512)S(1)}, f32[512]{0:T(512)S(1)}) all-reduce(f32[512]{0:T(512)S(1)} %get-tuple-element.198, f32[512]{0:T(512)S(1)} %get-tuple-element.197, f32[512]{0:T(512)S(1)} %get-tuple-element.196), channel_id=1, replica_groups=mesh['dp'=16,'code'=32] {'code'}, use_global_device_ids=true, to_apply=%region_10.11 | all-reduce | flops 1536 | bytes 12288 | tf_op jit(solution)/shard_map/psum | solution.py:58
  137.4 0.6 subtract_reduce_fusion
  138.0 24.0 %while.32 = (s32[]{:T(128)}, f32[512,256]{1,0:T(8,128)}, f32[4,1024]{1,0:T(4,128)S(1)}, f32[4,1024,256]{2,1,0:T(8,128)}, bf16[4,1024,256]{2,1,0:T(8,128)(2,1)}, ...) while((s32[]{:T(128)}, f32[512,256]{1,0:T(8,128)}, ...), condition=%wide.region_15.16_spmd.clone, body=%wide.region_13.15_spmd.clone.sunk | while | flops 1077935104 | bytes 22300912 | solution.py:79
  138.0 1.9 fusion.64
  140.0 0.5 multiply_convert_fusion.3
  140.5 0.1 dynamic_update_slice.35
  140.6 1.2 convolution_add_fusion.2
  141.8 1.5 fusion.65
  143.3 1.9 fusion.64
  145.2 0.5 multiply_convert_fusion.3
  145.7 0.1 dynamic_update_slice.35
  145.8 2.3 convolution_add_fusion.2
  148.1 1.4 fusion.65
  149.5 1.9 fusion.64
  151.5 0.5 multiply_convert_fusion.3
  152.0 0.1 dynamic_update_slice.35
  152.0 2.3 convolution_add_fusion.2
  154.3 1.5 fusion.65
  155.8 1.9 fusion.64
  157.7 0.5 multiply_convert_fusion.3
  158.2 0.1 dynamic_update_slice.35
  158.3 2.3 convolution_add_fusion.2
  160.6 1.4 fusion.65
  162.1 0.0 all-gather.2.cloned.1.call-start
  162.2 3.4 gather_fusion
  165.6 0.9 select_convert_fusion
  166.5 0.0 reduce-scatter.2.cloned.1.call-start
  166.6 6.3 %scatter_custom_fusion = f32[4097,256]{1,0:T(8,128)} fusion(s32[512]{0:T(512)S(1)} %subtract_select_fusion, f32[]{:T(128)} %constant.47.clone.1, bf16[512,256]{1,0:T(8,128)(2,1)S(1)} %copy-done.3), kind=kCustom, calls=%fused_computation.34 | custom fusion | flops 262144 | bytes 4457476 | tf_op jit(solution)/shard_map/scatter-add | solution.py:22
  172.9 5.2 %fusion.22 = bf16[4096,256]{1,0:T(8,128)(2,1)} fusion(f32[4097,256]{1,0:T(8,128)} %scatter_custom_fusion, f32[4,1024,256]{2,1,0:T(8,128)} %get-tuple-element.108), kind=kLoop, calls=%fused_computation.33 | loop fusion | flops 2097152 | bytes 10485760 | tf_op jit(solution)/shard_map/convert_element_type | solution.py:85
  178.2 1.3 dynamic-slice
  180.7 73.5 %all-reduce = f32[4096]{0:T(1024)S(1)} all-reduce(f32[4096]{0:T(1024)S(1)} %bitcast.109), channel_id=3, replica_groups=mesh['dp'=16,'code'=32] {'dp'}, use_global_device_ids=true, to_apply=%region_19.20.clone | all-reduce | flops 4096 | bytes 32768
  254.2 1.2 fusion.26
  256.1 106.5 %psum.39 = f32[]{:T(128)} all-reduce(f32[]{:T(128)S(6)} %add.43), channel_id=1, replica_groups=mesh['dp'=16,'code'=32] {'dp','code'}, use_global_device_ids=true, to_apply=%region_24.25 | all-reduce | flops 1 | bytes 8 | tf_op jit(solution)/shard_map/psum | solution.py:96
  362.6 29.0 %all-reduce.4.cloned.1.call-done = f32[512,256]{1,0:T(8,128)} async-done(((f32[512,256]{1,0:T(8,128)}), f32[512,256]{1,0:T(8,128)}) %all-reduce.4.cloned.1.call-update) | async-done | bytes 524304 | tf_op jit(solution)/shard_map/psum | solution.py:88
  391.6 1.8 multiply_convert_fusion.1
  393.4 74.7 %all-gather.2.cloned.1.call-done = bf16[32,512,256]{2,1,0:T(8,128)(2,1)} async-done(((bf16[1,512,256]{2,1,0:T(8,128)(2,1)}), bf16[32,512,256]{2,1,0:T(8,128)(2,1)}) %all-gather.2.cloned.1.call-update) | async-done | bytes 8388624 | tf_op jit(solution)/shard_map/all_gather | solution.py:21
  468.1 5.5 %reduce_sum.93 = bf16[512,256]{1,0:T(8,128)(2,1)} reduce(bf16[32,512,256]{2,1,0:T(8,128)(2,1)} %all-gather.2.cloned.1.call-done, bf16[]{:T(256)} %constant.48.clone.1), dimensions={0}, to_apply=%region_0.1 | reduce | flops 4063232 | bytes 8650754 | tf_op jit(solution)/shard_map/reduce_sum | solution.py:21
  (58 shorter events, 0.4 us)
Async XLA Ops:
  8.0 383.6 %all-reduce.4.cloned.1.call-start = ((), (), s32[]{:S(2)}) async-start(), calls=%async_computation.2 | async-start | bytes 1048576 | tf_op jit(solution)/shard_map/psum | solution.py:88
  8.1 1.6 copy-start.1
  12.1 1.6 copy-start.1
  16.2 1.6 copy-start.1
  20.2 1.7 copy-start.1
  138.0 24.1 %copy-start.5 = (s32[512]{0:T(512)S(1)}, s32[512]{0:T(512)}, u32[]{:S(2)}) copy-start(s32[512]{0:T(512)} %param.11) | copy-start | bytes 6148
  138.0 1.9 copy-start
  138.0 1.9 copy-start.2
  140.5 1.3 copy-start.4
  143.3 1.9 copy-start
  143.3 1.9 copy-start.2
  145.7 2.4 copy-start.4
  149.5 1.9 copy-start
  149.5 1.9 copy-start.2
  151.9 2.4 copy-start.4
  155.8 1.9 copy-start
  155.8 1.9 copy-start.2
  158.2 2.4 copy-start.4
  162.0 4.6 copy-start.3
  162.1 306.0 %all-gather.2.cloned.1.call-start = ((), (), s32[]{:S(2)}) async-start(), calls=%async_computation.1 | async-start | bytes 8650752 | tf_op jit(solution)/shard_map/all_gather | solution.py:21
  166.5 307.0 %reduce-scatter.2.cloned.1.call-start = ((), (), s32[]{:S(2)}) async-start(), calls=%async_computation.3 | async-start | bytes 2228224 | tf_op jit(solution)/shard_map/reduce_scatter | solution.py:84
Sparse Core Ops, SparseCore 0:
  162.2 229.3 all-reduce.3
  394.3 73.7 all-gather.1
Sparse Core Ops, SparseCore 1:
  178.2 91.8 reduce-scatter.1
